TPU v7x, 256 devices: a whole 4x4x8 slice. The times are simulated.
256 devices in a mesh: pair: 16 (over z, core), red: 16 (over x, y).
Axes of the slice: x: 4, y: 4, z: 8, core: 2. Of those that a mesh axis runs over, the one named last changes fastest.
Arguments:
- three_center: bfloat16 [2304, 256, 256], P('pair', 'red'), may hold values from -0.375 to 0.375
- occ_src: int32 [256, 16], P('red'), may hold values from 0 to 15, as said below
- occ_block: int32 [256, 16], P('red'), may hold values from 0 to 31
- occ_blocks: bfloat16 [512, 256], P('red'), may hold values from -0.375 to 0.375
- virt_block: int32 [16, 16, 1], P('red'), may hold values from 0 to 31, as said below
- virt_blocks: bfloat16 [16, 32, 256], P('red', 'pair'), may hold values from -1.5 to 1.5
Outputs:
- chi: float32 [2304, 2304], P('pair', 'red')
Inputs may be any that keep to these rules, and one draw needn't show every extreme that they name: `occ_src`: the 16 entries of a row are distinct. `virt_block`: every block listed for tile t of a red group lies from (t) * 2 to (t) * 2 + 1.
All inputs are finite; a program needn't handle non-finite values.
Results may differ from a plain program's by a relative error of at most 0.0041.
Values may be sent and summed in bfloat16 or wider, within the bound.
A program may use at most 128 MiB of HBM per device.

v0:
```python
import jax
import jax.numpy as jnp
from jax import lax
from jax.sharding import PartitionSpec as P

BLK = 16
TPD = 1


def occupied(three_center, occ_src, occ_block, occ_blocks):
    aux_rows, ntiles, area = three_center.shape
    nblocks = occ_blocks.shape[0]
    block_hot = (
        occ_block[:, :, None] == jnp.arange(nblocks, dtype=jnp.int32)[None, None, :]
    ).astype(jnp.bfloat16)
    picked = jnp.einsum(
        "tsb,bk->tsk", block_hot, occ_blocks, preferred_element_type=jnp.float32
    ).astype(jnp.bfloat16)
    source_hot = (occ_src[:, :, None] == jnp.arange(ntiles, dtype=jnp.int32)[None, None, :]).astype(
        jnp.bfloat16
    )
    mixing = jnp.einsum(
        "tsk,tsa->tka", source_hot, picked, preferred_element_type=jnp.float32
    ).astype(jnp.bfloat16)
    mixing = mixing.reshape(ntiles, ntiles, BLK, BLK)
    blocks = three_center.reshape(aux_rows, ntiles, BLK, BLK)
    half = jnp.einsum("tkml,pkln->ptmn", mixing, blocks, preferred_element_type=jnp.float32)
    return half.reshape(aux_rows, ntiles, area).astype(jnp.bfloat16)


def virtual(half, listed, blocks):
    aux_rows, ntiles, area = half.shape
    owners = listed.shape[0]
    nblocks = blocks.shape[0]
    block_hot = (listed[..., None] == jnp.arange(nblocks, dtype=jnp.int32)).astype(jnp.bfloat16)
    picked = jnp.einsum(
        "oijb,bk->oijk", block_hot, blocks, preferred_element_type=jnp.float32
    ).astype(jnp.bfloat16)
    picked = picked.reshape(owners, TPD, TPD, BLK, BLK)
    grouped = half.reshape(aux_rows, owners, TPD, BLK, BLK)
    kernel = jnp.einsum("pojml,oijln->poimn", grouped, picked, preferred_element_type=jnp.float32)
    return kernel.reshape(aux_rows, ntiles, area).astype(jnp.bfloat16)


def shards(three_center, occ_src, occ_block, occ_blocks, virt_block, virt_blocks):
    aux_rows, ntiles, area = three_center.shape
    half = occupied(three_center, occ_src, occ_block, occ_blocks)
    own_blocks = virt_blocks[0]
    listed = virt_block[0]
    all_blocks = lax.all_gather(own_blocks, "pair", axis=0, tiled=True)
    kernel = virtual(half, listed.reshape(ntiles // TPD, TPD, TPD), all_blocks)
    flat_tiles = three_center.reshape(aux_rows, ntiles * area)
    piece = lax.all_gather(kernel, "pair", axis=0, tiled=True)
    flat_piece = piece.reshape(piece.shape[0], ntiles * area)
    partial_value = lax.dot_general(
        flat_tiles, flat_piece, (((1,), (1,)), ((), ())), preferred_element_type=jnp.float32
    )
    return lax.psum_scatter(partial_value, "red", scatter_dimension=1, tiled=True)


def solution(mesh):
    placed = (
        P("pair", "red", None),
        P("red", None),
        P("red", None),
        P("red", None),
        P("red", None, None),
        P("red", "pair", None),
    )
    return jax.shard_map(
        shards, mesh=mesh, in_specs=placed, out_specs=P("pair", "red"), check_vma=False
    )
```

profile of v0, /device:TPU:32, one launch (start us, length us, event | category | flops | bytes accessed | tf_op | source)
XLA Modules:
  0.0 243.4 jit_solution(1345893647742258906)
XLA Ops:
  6.5 0.0 copy-start
  6.5 0.0 copy-start.1
  6.5 0.0 all-gather.3.cloned.1.call-start
  6.5 0.8 copy.21
  7.3 17.9 %all-gather = bf16[1,32,256]{2,0,1:T(2,128)(2,1)S(1)} all-gather(bf16[1,2,256]{2,0,1:T(2,128)(2,1)S(1)} %copy.21), channel_id=2, replica_groups=mesh['pair'=16,'red'=16] {'pair'}, dimensions={1}, use_global_device_ids=true | all-gather | bytes 17408 | tf_op jit(solution)/shard_map/all_gather | solution.py:50
  25.2 0.8 convolution_convert_fusion.2
  26.1 0.1 reshape.42
  26.2 0.0 copy-done
  26.2 1.1 convolution_convert_fusion
  27.3 1.7 reshape.47
  29.0 0.0 copy-done.1
  29.0 1.2 copy.22
  30.2 3.4 %fusion.7 = bf16[144,16,16,16]{0,2,3,1:T(8,128)(2,1)S(1)} fusion(bf16[144,16,16,16]{0,3,2,1:T(8,128)(2,1)S(1)} %bitcast.43, bf16[16,16,16,16,1]{3,2,1,0,4:T(8,128)(2,1)} %reshape.47), kind=kOutput, calls=%fused_computation.7 | convolution fusion | flops 302579712 | bytes 2490368 | tf_op jit(solution)/shard_map/tkml,pkln->ptmn/dot_general | solution.py:27
  33.5 2.2 fusion.4
  35.7 3.7 %copy.26 = bf16[144,16,256]{2,0,1:T(8,128)(2,1)} copy(bf16[144,16,256]{0,2,1:T(8,128)(2,1)} %bitcast.44) | data formatting | bytes 2359296 | tf_op jit(solution)/shard_map/convert_element_type | solution.py:42
  39.4 0.0 all-gather.3.cloned.1.call-update
  39.4 0.0 reduce-scatter.4.cloned.1.call-start
  39.5 103.4 %all-gather.3.cloned.1.call-done = bf16[2304,16,256]{2,0,1:T(8,128)(2,1)} async-done(((bf16[144,16,256]{2,0,1:T(8,128)(2,1)}), bf16[2304,16,256]{2,0,1:T(8,128)(2,1)}) %all-gather.3.cloned.1.call-update) | async-done | bytes 18874384 | tf_op jit(solution)/shard_map/all_gather | solution.py:53
  142.8 9.5 %convolution_bitcast_fusion = f32[144,2304]{1,0:T(8,128)S(1)} fusion(bf16[2304,16,256]{2,0,1:T(8,128)(2,1)} %all-gather.3.cloned.1.call-done, bf16[144,16,256]{0,2,1:T(8,128)(2,1)S(1)} %copy.22), kind=kOutput, calls=%fused_computation.1 | convolution fusion | flops 2717908992 | bytes 21381120 | tf_op jit(solution)/shard_map/dot_general | solution.py:55
  152.3 1.9 copy.33
  154.2 0.0 reduce-scatter.4.cloned.1.call-update
  154.3 80.6 %reduce-scatter.4.cloned.1.call-done = f32[144,144]{1,0:T(8,128)} async-done(((f32[2304,144]{1,0:T(8,128)}), f32[144,144]{1,0:T(8,128)}) %reduce-scatter.4.cloned.1.call-update) | async-done | bytes 82960
  234.9 1.7 copy.34
Async XLA Ops:
  6.5 19.6 %copy-start = (bf16[32,256]{1,0:T(8,128)(2,1)S(1)}, bf16[32,256]{1,0:T(8,128)(2,1)}, u32[]{:S(2)}) copy-start(bf16[32,256]{1,0:T(8,128)(2,1)} %param.9) | copy-start | bytes 49156
  6.5 22.4 %copy-start.1 = (bf16[144,16,256]{2,1,0:T(8,128)(2,1)S(1)}, bf16[144,16,256]{2,1,0:T(8,128)(2,1)}, u32[]{:S(2)}) copy-start(bf16[144,16,256]{2,1,0:T(8,128)(2,1)} %param.6) | copy-start | bytes 3538948
  6.5 136.3 %all-gather.3.cloned.1.call-start = ((), (), s32[]{:S(2)}) async-start(), calls=%async_computation.1 | async-start | bytes 20054016 | tf_op jit(solution)/shard_map/all_gather | solution.py:53
  39.4 195.4 %reduce-scatter.4.cloned.1.call-start = ((), (), s32[]{:S(2)}) async-start(), calls=%async_computation.2 | async-start | bytes 2506752
Sparse Core Ops, SparseCore 0:
  39.6 103.2 all-gather.2
  154.4 80.4 reduce-scatter.3
where the time goes:
time: 244 us; the launch traced here: 243 us
  waiting for transfers between devices  184 us (75%)
  blocking collectives  17.9 us (7%)
  matrix products  17 us (7%)
  between operations  13.4 us (5%)
  local copies, waits for them, and re-layouts  11 us (5%)
    all_gather x1, waiting for transfers between devices, shards(): piece = lax.all_gather(kernel, 'pair', axis=0, tiled=True)  103 us
    unnamed x3, waiting for transfers between devices  80.6 us
    all_gather x1, blocking collectives, shards(): all_blocks = lax.all_gather(own_blocks, 'pair', axis=0, tiled=True)  17.9 us
    dot_general x1, matrix products, shards(): lax.dot_general(flat_tiles, flat_piece, (((1,), (1,)), ((), ())), preferr...  9.48 us
    unnamed x8, local copies, waits for them, and re-layouts  5.55 us
  transfers between devices with their start and end apart: 2, of which 2 were waited for; matrix products, arithmetic and copies ran while one was open for 0% of the time, Pallas kernels for 0%

commit v1 on v0

--- a/solution.py
+++ b/solution.py
@@ -47,7 +47,12 @@
     half = occupied(three_center, occ_src, occ_block, occ_blocks)
     own_blocks = virt_blocks[0]
     listed = virt_block[0]
-    all_blocks = lax.all_gather(own_blocks, "pair", axis=0, tiled=True)
+    ring = [own_blocks]
+    for hop in range(15):
+        ring.append(lax.ppermute(ring[-1], "pair", [(dev, (dev + 1) % 16) for dev in range(16)]))
+    all_blocks = jnp.roll(
+        jnp.concatenate(ring[::-1], axis=0), (lax.axis_index("pair") + 1) * ring[0].shape[0], axis=0
+    )
     kernel = virtual(half, listed.reshape(ntiles // TPD, TPD, TPD), all_blocks)
     flat_tiles = three_center.reshape(aux_rows, ntiles * area)
     piece = lax.all_gather(kernel, "pair", axis=0, tiled=True)

time: 244 us -> 285 us (1.17)
  waiting for transfers between devices: 184 us -> 241 us
  blocking collectives: 17.9 us -> 0 us
    ppermute x0 -> x15, waiting for transfers between devices: none -> 50.4 us  [shards(): lax.ppermute(ring[-1], 'pair', [(dev, (dev + 1) % 16) for dev in range(16)])]
    all_gather x1 -> x0, blocking collectives: 17.9 us -> none  [shards(): all_blocks = lax.all_gather(own_blocks, 'pair', axis=0, tiled=True)]
    all_gather x1, waiting for transfers between devices: 103 us -> 110 us  [shards(): piece = lax.all_gather(kernel, 'pair', axis=0, tiled=True)]
  transfers between devices with their start and end apart: 2 -> 17, of which waited for: 2 -> 16; matrix products, arithmetic and copies ran while one was open for 0% -> 3% of each run, Pallas kernels for 0% -> 0%
where the time goes in v1:
time: 285 us
  waiting for transfers between devices  241 us (85%)
  matrix products  18.9 us (7%)
  between operations  13.5 us (5%)
  local copies, waits for them, and re-layouts  10.4 us (4%)
    all_gather x1, waiting for transfers between devices, shards(): piece = lax.all_gather(kernel, 'pair', axis=0, tiled=True)  110 us
    unnamed x3, waiting for transfers between devices  80.6 us
    ppermute x15, waiting for transfers between devices, shards(): lax.ppermute(ring[-1], 'pair', [(dev, (dev + 1) % 16) for dev in range(16)])  50.4 us
    dot_general x1, matrix products, shards(): lax.dot_general(flat_tiles, flat_piece, (((1,), (1,)), ((), ())), preferr...  9.48 us
  transfers between devices with their start and end apart: 17, of which 16 were waited for; matrix products, arithmetic and copies ran while one was open for 3% of the time, Pallas kernels for 0%

profile of v1, /device:TPU:32, one launch (start us, length us, event | category | flops | bytes accessed | tf_op | source)
XLA Modules:
  0.0 284.5 jit_solution(15458300502801408502)
XLA Ops:
  6.5 0.0 collective-permute-start
  6.6 3.2 %collective-permute-done = bf16[2,256]{1,0:T(2,128)(2,1)S(1)} collective-permute-done((bf16[2,256]{1,0:T(2,128)(2,1)}, bf16[2,256]{1,0:T(2,128)(2,1)S(1)}, u32[]{:S(2)}, u32[]{:S(2)}) %collective-permute-start) | collective-permute-done | bytes 1056 | tf_op jit(solution)/shard_map/ppermute | solution.py:52
  9.7 0.0 collective-permute-start.1
  9.8 3.0 %collective-permute-done.1 = bf16[2,256]{1,0:T(2,128)(2,1)S(1)} collective-permute-done((bf16[2,256]{1,0:T(2,128)(2,1)S(1)}, bf16[2,256]{1,0:T(2,128)(2,1)S(1)}, u32[]{:S(2)}, u32[]{:S(2)}) %collective-permute-start.1) | collective-permute-done | bytes 1056 | tf_op jit(solution)/shard_map/ppermute | solution.py:52
  12.7 0.0 collective-permute-start.2
  12.7 3.0 %collective-permute-done.2 = bf16[2,256]{1,0:T(2,128)(2,1)S(1)} collective-permute-done((bf16[2,256]{1,0:T(2,128)(2,1)S(1)}, bf16[2,256]{1,0:T(2,128)(2,1)S(1)}, u32[]{:S(2)}, u32[]{:S(2)}) %collective-permute-start.2) | collective-permute-done | bytes 1056 | tf_op jit(solution)/shard_map/ppermute | solution.py:52
  15.7 0.0 collective-permute-start.3
  15.7 3.9 %collective-permute-done.3 = bf16[2,256]{1,0:T(2,128)(2,1)S(1)} collective-permute-done((bf16[2,256]{1,0:T(2,128)(2,1)S(1)}, bf16[2,256]{1,0:T(2,128)(2,1)S(1)}, u32[]{:S(2)}, u32[]{:S(2)}) %collective-permute-start.3) | collective-permute-done | bytes 1056 | tf_op jit(solution)/shard_map/ppermute | solution.py:52
  19.6 0.0 collective-permute-start.4
  19.6 4.2 %collective-permute-done.4 = bf16[2,256]{1,0:T(2,128)(2,1)S(1)} collective-permute-done((bf16[2,256]{1,0:T(2,128)(2,1)S(1)}, bf16[2,256]{1,0:T(2,128)(2,1)S(1)}, u32[]{:S(2)}, u32[]{:S(2)}) %collective-permute-start.4) | collective-permute-done | bytes 1056 | tf_op jit(solution)/shard_map/ppermute | solution.py:52
  23.8 0.0 collective-permute-start.5
  23.8 4.2 %collective-permute-done.5 = bf16[2,256]{1,0:T(2,128)(2,1)S(1)} collective-permute-done((bf16[2,256]{1,0:T(2,128)(2,1)S(1)}, bf16[2,256]{1,0:T(2,128)(2,1)S(1)}, u32[]{:S(2)}, u32[]{:S(2)}) %collective-permute-start.5) | collective-permute-done | bytes 1056 | tf_op jit(solution)/shard_map/ppermute | solution.py:52
  28.0 0.0 collective-permute-start.6
  28.0 4.2 %collective-permute-done.6 = bf16[2,256]{1,0:T(2,128)(2,1)S(1)} collective-permute-done((bf16[2,256]{1,0:T(2,128)(2,1)S(1)}, bf16[2,256]{1,0:T(2,128)(2,1)S(1)}, u32[]{:S(2)}, u32[]{:S(2)}) %collective-permute-start.6) | collective-permute-done | bytes 1056 | tf_op jit(solution)/shard_map/ppermute | solution.py:52
  32.2 0.0 collective-permute-start.7
  32.2 4.2 %collective-permute-done.7 = bf16[2,256]{1,0:T(2,128)(2,1)S(1)} collective-permute-done((bf16[2,256]{1,0:T(2,128)(2,1)S(1)}, bf16[2,256]{1,0:T(2,128)(2,1)S(1)}, u32[]{:S(2)}, u32[]{:S(2)}) %collective-permute-start.7) | collective-permute-done | bytes 1056 | tf_op jit(solution)/shard_map/ppermute | solution.py:52
  36.4 0.0 collective-permute-start.8
  36.4 4.2 %collective-permute-done.8 = bf16[2,256]{1,0:T(2,128)(2,1)S(1)} collective-permute-done((bf16[2,256]{1,0:T(2,128)(2,1)S(1)}, bf16[2,256]{1,0:T(2,128)(2,1)S(1)}, u32[]{:S(2)}, u32[]{:S(2)}) %collective-permute-start.8) | collective-permute-done | bytes 1056 | tf_op jit(solution)/shard_map/ppermute | solution.py:52
  40.6 0.0 collective-permute-start.9
  40.6 4.2 %collective-permute-done.9 = bf16[2,256]{1,0:T(2,128)(2,1)S(1)} collective-permute-done((bf16[2,256]{1,0:T(2,128)(2,1)S(1)}, bf16[2,256]{1,0:T(2,128)(2,1)S(1)}, u32[]{:S(2)}, u32[]{:S(2)}) %collective-permute-start.9) | collective-permute-done | bytes 1056 | tf_op jit(solution)/shard_map/ppermute | solution.py:52
  44.8 0.0 collective-permute-start.10
  44.8 4.2 %collective-permute-done.10 = bf16[2,256]{1,0:T(2,128)(2,1)S(1)} collective-permute-done((bf16[2,256]{1,0:T(2,128)(2,1)S(1)}, bf16[2,256]{1,0:T(2,128)(2,1)S(1)}, u32[]{:S(2)}, u32[]{:S(2)}) %collective-permute-start.10) | collective-permute-done | bytes 1056 | tf_op jit(solution)/shard_map/ppermute | solution.py:52
  49.1 0.0 collective-permute-start.11
  49.1 4.2 %collective-permute-done.11 = bf16[2,256]{1,0:T(2,128)(2,1)S(1)} collective-permute-done((bf16[2,256]{1,0:T(2,128)(2,1)S(1)}, bf16[2,256]{1,0:T(2,128)(2,1)S(1)}, u32[]{:S(2)}, u32[]{:S(2)}) %collective-permute-start.11) | collective-permute-done | bytes 1056 | tf_op jit(solution)/shard_map/ppermute | solution.py:52
  53.3 0.0 collective-permute-start.12
  53.3 1.1 convolution_convert_fusion
  54.3 1.7 reshape.46
  56.0 1.2 copy.14
  57.2 0.2 collective-permute-done.12
  57.5 0.0 collective-permute-start.13
  57.5 4.4 %fusion.7 = bf16[144,16,16,16]{0,2,3,1:T(8,128)(2,1)} fusion(bf16[144,16,16,16]{0,3,2,1:T(8,128)(2,1)S(1)} %bitcast.41, bf16[16,16,16,16,1]{3,2,1,0,4:T(8,128)(2,1)} %reshape.46), kind=kOutput, calls=%fused_computation.7 | convolution fusion | flops 302579712 | bytes 2490368 | tf_op jit(solution)/shard_map/tkml,pkln->ptmn/dot_general | solution.py:27
  61.8 0.0 collective-permute-done.13
  61.9 0.7 collective-permute-start.14
  62.6 3.5 %collective-permute-done.14 = bf16[2,256]{1,0:T(2,128)(2,1)S(1)} collective-permute-done((bf16[2,256]{1,0:T(2,128)(2,1)S(1)}, bf16[2,256]{1,0:T(2,128)(2,1)S(1)}, u32[]{:S(2)}, u32[]{:S(2)}) %collective-permute-start.14) | collective-permute-done | bytes 1056 | tf_op jit(solution)/shard_map/ppermute | solution.py:52
  66.1 0.0 copy-done.2
  66.1 0.2 concatenate.6
  66.2 0.2 convolution_convert_fusion.2
  66.4 0.1 reshape.42
  66.5 3.7 %fusion.4 = bf16[16,16,144,16]{2,1,3,0:T(8,128)(2,1)} fusion(bf16[144,16,16,16]{0,2,3,1:T(8,128)(2,1)} %fusion.7, bf16[16,16,16]{2,1,0:T(8,128)(2,1)S(1)} %reshape.42), kind=kOutput, calls=%fused_computation.6 | convolution fusion | flops 19464192 | bytes 2367488 | tf_op jit(solution)/shard_map/pojml,oijln->poimn/dot_general | solution.py:41
  70.3 3.6 %copy.18 = bf16[144,16,256]{2,0,1:T(8,128)(2,1)} copy(bf16[144,16,256]{0,2,1:T(8,128)(2,1)} %bitcast.42) | data formatting | bytes 2359296 | tf_op jit(solution)/shard_map/convert_element_type | solution.py:42
  73.9 0.0 all-gather.2.cloned.1.call-update
  74.0 0.0 reduce-scatter.4.cloned.1.call-start
  74.0 110.0 %all-gather.2.cloned.1.call-done = bf16[2304,16,256]{2,0,1:T(8,128)(2,1)} async-done(((bf16[144,16,256]{2,0,1:T(8,128)(2,1)}), bf16[2304,16,256]{2,0,1:T(8,128)(2,1)}) %all-gather.2.cloned.1.call-update) | async-done | bytes 18874384 | tf_op jit(solution)/shard_map/all_gather | solution.py:58
  184.0 9.5 %convolution_bitcast_fusion = f32[144,2304]{1,0:T(8,128)S(1)} fusion(bf16[2304,16,256]{2,0,1:T(8,128)(2,1)} %all-gather.2.cloned.1.call-done, bf16[144,16,256]{0,2,1:T(8,128)(2,1)S(1)} %copy.14), kind=kOutput, calls=%fused_computation.1 | convolution fusion | flops 2717908992 | bytes 21381120 | tf_op jit(solution)/shard_map/dot_general | solution.py:60
  193.5 1.9 copy.25
  195.4 0.0 reduce-scatter.4.cloned.1.call-update
  195.5 80.6 %reduce-scatter.4.cloned.1.call-done = f32[144,144]{1,0:T(8,128)} async-done(((f32[2304,144]{1,0:T(8,128)}), f32[144,144]{1,0:T(8,128)}) %reduce-scatter.4.cloned.1.call-update) | async-done | bytes 82960
  276.0 1.7 copy.26
  (8 shorter events, 0.0 us)
Async XLA Ops:
  6.5 46.7 %copy-start = (bf16[32,256]{1,0:T(8,128)(2,1)S(1)}, bf16[32,256]{1,0:T(8,128)(2,1)}, u32[]{:S(2)}) copy-start(bf16[32,256]{1,0:T(8,128)(2,1)} %param.9) | copy-start | bytes 49156
  6.5 49.5 %copy-start.1 = (bf16[144,16,256]{2,1,0:T(8,128)(2,1)S(1)}, bf16[144,16,256]{2,1,0:T(8,128)(2,1)}, u32[]{:S(2)}) copy-start(bf16[144,16,256]{2,1,0:T(8,128)(2,1)} %param.6) | copy-start | bytes 3538948
  6.5 177.5 %all-gather.2.cloned.1.call-start = ((), (), s32[]{:S(2)}) async-start(), calls=%async_computation.1 | async-start | bytes 20054016 | tf_op jit(solution)/shard_map/all_gather | solution.py:58
  6.5 3.2 %collective-permute-start = (bf16[2,256]{1,0:T(2,128)(2,1)}, bf16[2,256]{1,0:T(2,128)(2,1)S(1)}, u32[]{:S(2)}, u32[]{:S(2)}) collective-permute-start(bf16[2,256]{1,0:T(2,128)(2,1)} %bitcast.44), channel_id=1, source_target_pairs={{0,16},{16,32},{32,48},{48,64},{64,80},{80,96},{96,112},{112,128},... | collective-permute-start | bytes 3080 | tf_op jit(solution)/shard_map/ppermute | solution.py:52
  9.7 3.0 %collective-permute-start.1 = (bf16[2,256]{1,0:T(2,128)(2,1)S(1)}, bf16[2,256]{1,0:T(2,128)(2,1)S(1)}, u32[]{:S(2)}, u32[]{:S(2)}) collective-permute-start(bf16[2,256]{1,0:T(2,128)(2,1)S(1)} %collective-permute-done), channel_id=1, source_target_pairs={{0,16},{16,32},{32,48},{48,64},{64,80},{80,96},{96,112},{112,128},... | collective-permute-start | bytes 3080 | tf_op jit(solution)/shard_map/ppermute | solution.py:52
  12.7 3.0 %collective-permute-start.2 = (bf16[2,256]{1,0:T(2,128)(2,1)S(1)}, bf16[2,256]{1,0:T(2,128)(2,1)S(1)}, u32[]{:S(2)}, u32[]{:S(2)}) collective-permute-start(bf16[2,256]{1,0:T(2,128)(2,1)S(1)} %collective-permute-done.1), channel_id=1, source_target_pairs={{0,16},{16,32},{32,48},{48,64},{64,80},{80,96},{96,112},{112,128},... | collective-permute-start | bytes 3080 | tf_op jit(solution)/shard_map/ppermute | solution.py:52
  15.7 3.9 %collective-permute-start.3 = (bf16[2,256]{1,0:T(2,128)(2,1)S(1)}, bf16[2,256]{1,0:T(2,128)(2,1)S(1)}, u32[]{:S(2)}, u32[]{:S(2)}) collective-permute-start(bf16[2,256]{1,0:T(2,128)(2,1)S(1)} %collective-permute-done.2), channel_id=1, source_target_pairs={{0,16},{16,32},{32,48},{48,64},{64,80},{80,96},{96,112},{112,128},... | collective-permute-start | bytes 3080 | tf_op jit(solution)/shard_map/ppermute | solution.py:52
  19.6 4.2 %collective-permute-start.4 = (bf16[2,256]{1,0:T(2,128)(2,1)S(1)}, bf16[2,256]{1,0:T(2,128)(2,1)S(1)}, u32[]{:S(2)}, u32[]{:S(2)}) collective-permute-start(bf16[2,256]{1,0:T(2,128)(2,1)S(1)} %collective-permute-done.3), channel_id=1, source_target_pairs={{0,16},{16,32},{32,48},{48,64},{64,80},{80,96},{96,112},{112,128},... | collective-permute-start | bytes 3080 | tf_op jit(solution)/shard_map/ppermute | solution.py:52
  23.8 4.2 %collective-permute-start.5 = (bf16[2,256]{1,0:T(2,128)(2,1)S(1)}, bf16[2,256]{1,0:T(2,128)(2,1)S(1)}, u32[]{:S(2)}, u32[]{:S(2)}) collective-permute-start(bf16[2,256]{1,0:T(2,128)(2,1)S(1)} %collective-permute-done.4), channel_id=1, source_target_pairs={{0,16},{16,32},{32,48},{48,64},{64,80},{80,96},{96,112},{112,128},... | collective-permute-start | bytes 3080 | tf_op jit(solution)/shard_map/ppermute | solution.py:52
  28.0 4.2 %collective-permute-start.6 = (bf16[2,256]{1,0:T(2,128)(2,1)S(1)}, bf16[2,256]{1,0:T(2,128)(2,1)S(1)}, u32[]{:S(2)}, u32[]{:S(2)}) collective-permute-start(bf16[2,256]{1,0:T(2,128)(2,1)S(1)} %collective-permute-done.5), channel_id=1, source_target_pairs={{0,16},{16,32},{32,48},{48,64},{64,80},{80,96},{96,112},{112,128},... | collective-permute-start | bytes 3080 | tf_op jit(solution)/shard_map/ppermute | solution.py:52
  32.2 4.2 %collective-permute-start.7 = (bf16[2,256]{1,0:T(2,128)(2,1)S(1)}, bf16[2,256]{1,0:T(2,128)(2,1)S(1)}, u32[]{:S(2)}, u32[]{:S(2)}) collective-permute-start(bf16[2,256]{1,0:T(2,128)(2,1)S(1)} %collective-permute-done.6), channel_id=1, source_target_pairs={{0,16},{16,32},{32,48},{48,64},{64,80},{80,96},{96,112},{112,128},... | collective-permute-start | bytes 3080 | tf_op jit(solution)/shard_map/ppermute | solution.py:52
  36.4 4.2 %collective-permute-start.8 = (bf16[2,256]{1,0:T(2,128)(2,1)S(1)}, bf16[2,256]{1,0:T(2,128)(2,1)S(1)}, u32[]{:S(2)}, u32[]{:S(2)}) collective-permute-start(bf16[2,256]{1,0:T(2,128)(2,1)S(1)} %collective-permute-done.7), channel_id=1, source_target_pairs={{0,16},{16,32},{32,48},{48,64},{64,80},{80,96},{96,112},{112,128},... | collective-permute-start | bytes 3080 | tf_op jit(solution)/shard_map/ppermute | solution.py:52
  40.6 4.2 %collective-permute-start.9 = (bf16[2,256]{1,0:T(2,128)(2,1)S(1)}, bf16[2,256]{1,0:T(2,128)(2,1)S(1)}, u32[]{:S(2)}, u32[]{:S(2)}) collective-permute-start(bf16[2,256]{1,0:T(2,128)(2,1)S(1)} %collective-permute-done.8), channel_id=1, source_target_pairs={{0,16},{16,32},{32,48},{48,64},{64,80},{80,96},{96,112},{112,128},... | collective-permute-start | bytes 3080 | tf_op jit(solution)/shard_map/ppermute | solution.py:52
  44.8 4.2 %collective-permute-start.10 = (bf16[2,256]{1,0:T(2,128)(2,1)S(1)}, bf16[2,256]{1,0:T(2,128)(2,1)S(1)}, u32[]{:S(2)}, u32[]{:S(2)}) collective-permute-start(bf16[2,256]{1,0:T(2,128)(2,1)S(1)} %collective-permute-done.9), channel_id=1, source_target_pairs={{0,16},{16,32},{32,48},{48,64},{64,80},{80,96},{96,112},{112,128},... | collective-permute-start | bytes 3080 | tf_op jit(solution)/shard_map/ppermute | solution.py:52
  49.1 4.2 %collective-permute-start.11 = (bf16[2,256]{1,0:T(2,128)(2,1)S(1)}, bf16[2,256]{1,0:T(2,128)(2,1)S(1)}, u32[]{:S(2)}, u32[]{:S(2)}) collective-permute-start(bf16[2,256]{1,0:T(2,128)(2,1)S(1)} %collective-permute-done.10), channel_id=1, source_target_pairs={{0,16},{16,32},{32,48},{48,64},{64,80},{80,96},{96,112},{112,128},... | collective-permute-start | bytes 3080 | tf_op jit(solution)/shard_map/ppermute | solution.py:52
  53.3 4.2 %collective-permute-start.12 = (bf16[2,256]{1,0:T(2,128)(2,1)S(1)}, bf16[2,256]{1,0:T(2,128)(2,1)S(1)}, u32[]{:S(2)}, u32[]{:S(2)}) collective-permute-start(bf16[2,256]{1,0:T(2,128)(2,1)S(1)} %collective-permute-done.11), channel_id=1, source_target_pairs={{0,16},{16,32},{32,48},{48,64},{64,80},{80,96},{96,112},{112,128},... | collective-permute-start | bytes 3080 | tf_op jit(solution)/shard_map/ppermute | solution.py:52
  57.5 4.4 %collective-permute-start.13 = (bf16[2,256]{1,0:T(2,128)(2,1)S(1)}, bf16[2,256]{1,0:T(2,128)(2,1)S(1)}, u32[]{:S(2)}, u32[]{:S(2)}) collective-permute-start(bf16[2,256]{1,0:T(2,128)(2,1)S(1)} %collective-permute-done.12), channel_id=1, source_target_pairs={{0,16},{16,32},{32,48},{48,64},{64,80},{80,96},{96,112},{112,128},... | collective-permute-start | bytes 3080 | tf_op jit(solution)/shard_map/ppermute | solution.py:52
  57.5 8.6 %copy-start.2 = (bf16[1,2,256]{2,1,0:T(2,128)(2,1)S(1)}, bf16[1,2,256]{2,1,0:T(2,128)(2,1)}, u32[]{:S(2)}) copy-start(bf16[1,2,256]{2,1,0:T(2,128)(2,1)} %param.11) | copy-start | bytes 3076
  57.5 8.8 %copy-start.3 = (s32[1,16,1]{1,2,0:T(1,128)S(1)}, s32[1,16,1]{1,2,0:T(1,128)}, u32[]{:S(2)}) copy-start(s32[1,16,1]{1,2,0:T(1,128)} %param.10) | copy-start | bytes 196
  61.9 4.2 %collective-permute-start.14 = (bf16[2,256]{1,0:T(2,128)(2,1)S(1)}, bf16[2,256]{1,0:T(2,128)(2,1)S(1)}, u32[]{:S(2)}, u32[]{:S(2)}) collective-permute-start(bf16[2,256]{1,0:T(2,128)(2,1)S(1)} %collective-permute-done.13), channel_id=1, source_target_pairs={{0,16},{16,32},{32,48},{48,64},{64,80},{80,96},{96,112},{112,128},... | collective-permute-start | bytes 3080 | tf_op jit(solution)/shard_map/ppermute | solution.py:52
  74.0 202.1 %reduce-scatter.4.cloned.1.call-start = ((), (), s32[]{:S(2)}) async-start(), calls=%async_computation.2 | async-start | bytes 2506752
Sparse Core Ops, SparseCore 0:
  74.1 109.8 all-gather.1
  195.6 80.3 reduce-scatter.3
